TPU v7x, 256 devices: a whole 4x4x8 slice. The times are simulated.
256 devices in a mesh: gx: 32 (over y, z), gy: 8 (over x, core).
Axes of the slice: x: 4, y: 4, z: 8, core: 2. Of those that a mesh axis runs over, the one named last changes fastest.
Arguments:
- features: bfloat16 [2048, 64, 512], P(('gx', 'gy')), may hold values from -6 to 6
- neighbours: int32 [2048, 6], P(('gx', 'gy')), may hold values from 0 to 16, as said below
- counts: int32 [256], P(('gx', 'gy')), may hold values from 1 to 8, as said below
- conv_weight: bfloat16 [64, 448], replicated, may hold values from -0.25 to 0.25
- down_weight: bfloat16 [128, 512], replicated, may hold values from -0.25 to 0.25
- head_weight: bfloat16 [128, 128], replicated, may hold values from -0.5 to 0.5
- coarse_map: int32 [256, 8], P(('gx', 'gy')), may hold values from 0 to 32, as said below
- latent_grad: bfloat16 [256, 512, 128], P(('gx', 'gy')), may hold values from -6 to 6
Outputs:
- latent: bfloat16 [256, 512, 128], P(('gx', 'gy'))
- features_grad: bfloat16 [2048, 64, 512], P(('gx', 'gy'))
- conv_grad: float32 [64, 448], replicated
- down_grad: float32 [128, 512], replicated
- head_grad: float32 [128, 128], replicated
Inputs may be any that keep to these rules, and one draw needn't show every extreme that they name: `counts`: in every draw, max(1, (devices along gx times devices along gy) // 8) columns have exactly 8 active blocks; each other column has between 1 and 4. 16 means no neighbour; a value below 8 is an active slot of the same column; a value v of 8 or more is the active slot v - 8 of the adjacent column in that direction; the z directions never name another column; inactive slots have no neighbours. `coarse_map`: 32 marks an empty octant; every other entry names an active block's octant, and each such octant is named at most once among the four columns that share a merged list.
All inputs are finite; a program needn't handle non-finite values.
Results may differ from a plain program's by a relative error of at most 0.013.
Values may be sent and summed in bfloat16 or wider, within the bound.
A program may use at most 128 MiB of HBM per device.

v0:
```python
import jax
import jax.numpy as jnp
from jax import lax
from jax.sharding import PartitionSpec as P


def from_partner(block, axis, distance):
    count = lax.axis_size(axis)
    route = []
    for low in range(count):
        high = low | 1 << distance
        if high != low and high < count:
            route += [(low, high), (high, low)]
    return lax.ppermute(block, axis, route)


def padded(block, sides, width):
    for axis, dim in sides:
        count = lax.axis_size(axis)
        forward = [(i, i + 1) for i in range(count - 1)]
        backward = [(target, source) for source, target in forward]
        low = lax.ppermute(
            lax.slice_in_dim(block, block.shape[dim] - width, None, axis=dim), axis, forward
        )
        high = lax.ppermute(lax.slice_in_dim(block, 0, width, axis=dim), axis, backward)
        block = jnp.concatenate([low, block, high], axis=dim)
    return block


def silu_grad(values):
    sigmoid_value = jax.nn.sigmoid(values)
    return sigmoid_value * (1.0 + values * (1.0 - sigmoid_value))


def octet(volume):
    return volume.reshape(volume.shape[0], volume.shape[1], 2, 2, 2, 4, 4, 4)


def face_of(cube, axis_number, upper):
    number, channels = (cube.shape[0], cube.shape[1])
    plane = lax.index_in_dim(cube, 3 if upper else 0, 5 + axis_number, keepdims=False)
    plane = lax.index_in_dim(plane, 1 if upper else 0, 2 + axis_number, keepdims=False)
    return plane.reshape(number, channels * 64)


def face_index(axis_number, upper):
    index = [slice(None)] * 8
    index[2 + axis_number] = 1 if upper else 0
    index[5 + axis_number] = 3 if upper else 0
    return tuple(index)


def expand_plane(rows, cube, axis_number):
    number, channels = (cube.shape[0], cube.shape[1])
    return jnp.expand_dims(
        rows.reshape(number, channels, 2, 2, 4, 4), (2 + axis_number, 5 + axis_number)
    )


def shift_minus(cube, rows, axis_number):
    parity, place = (2 + axis_number, 5 + axis_number)
    plane = expand_plane(rows, cube, axis_number)
    lower = lax.slice_in_dim(cube, 0, 1, axis=parity)
    upper = lax.slice_in_dim(cube, 1, 2, axis=parity)
    out_low = jnp.concatenate([plane, lax.slice_in_dim(upper, 0, 3, axis=place)], axis=place)
    return jnp.concatenate([out_low, lower], axis=parity)


def shift_plus(cube, rows, axis_number):
    parity, place = (2 + axis_number, 5 + axis_number)
    plane = expand_plane(rows, cube, axis_number)
    lower = lax.slice_in_dim(cube, 0, 1, axis=parity)
    upper = lax.slice_in_dim(cube, 1, 2, axis=parity)
    out_high = jnp.concatenate([lax.slice_in_dim(lower, 1, 4, axis=place), plane], axis=place)
    return jnp.concatenate([upper, out_high], axis=parity)


def minus_back(grad_out, axis_number):
    parity, place = (2 + axis_number, 5 + axis_number)
    grad_low = lax.slice_in_dim(grad_out, 0, 1, axis=parity)
    grad_high = lax.slice_in_dim(grad_out, 1, 2, axis=parity)
    moved = jnp.concatenate(
        [
            lax.slice_in_dim(grad_low, 1, 4, axis=place),
            jnp.zeros_like(lax.slice_in_dim(grad_low, 0, 1, axis=place)),
        ],
        axis=place,
    )
    plane = lax.index_in_dim(
        lax.index_in_dim(grad_low, 0, place, keepdims=False), 0, parity, keepdims=False
    )
    return (jnp.concatenate([grad_high, moved], axis=parity), plane)


def plus_back(grad_out, axis_number):
    parity, place = (2 + axis_number, 5 + axis_number)
    grad_low = lax.slice_in_dim(grad_out, 0, 1, axis=parity)
    grad_high = lax.slice_in_dim(grad_out, 1, 2, axis=parity)
    moved = jnp.concatenate(
        [
            jnp.zeros_like(lax.slice_in_dim(grad_high, 0, 1, axis=place)),
            lax.slice_in_dim(grad_high, 0, 3, axis=place),
        ],
        axis=place,
    )
    plane = lax.index_in_dim(
        lax.index_in_dim(grad_high, 3, place, keepdims=False), 0, parity, keepdims=False
    )
    return (jnp.concatenate([moved, grad_low], axis=parity), plane)


def face_layers(cube):
    return (
        face_of(cube, 0, True),
        face_of(cube, 0, False),
        face_of(cube, 1, True),
        face_of(cube, 1, False),
        face_of(cube, 2, True),
        face_of(cube, 2, False),
    )


def pick_rows(local_rows, remote_rows, index):
    width = local_rows.shape[1]
    pooled = jnp.concatenate(
        [local_rows, remote_rows, jnp.zeros((1, width), local_rows.dtype)], axis=0
    )
    return pooled[index]


def neighbour_stack(cube, faces, remotes, links):
    number, channels = (cube.shape[0], cube.shape[1])
    blank = jnp.zeros_like(faces[4])
    sources = (remotes[0], remotes[1], remotes[2], remotes[3], blank, blank)
    picked = [
        pick_rows(faces[direction], sources[direction], links[:, direction])
        for direction in range(6)
    ]
    fields = [
        cube,
        shift_minus(cube, picked[0], 0),
        shift_plus(cube, picked[1], 0),
        shift_minus(cube, picked[2], 1),
        shift_plus(cube, picked[3], 1),
        shift_minus(cube, picked[4], 2),
        shift_plus(cube, picked[5], 2),
    ]
    return jnp.stack(fields, axis=1).reshape(number, 7 * channels, 512)


def stack_grad(taps_grad, links):
    number, channels = (taps_grad.shape[0], taps_grad.shape[1] // 7)
    parts = taps_grad.reshape(number, 7, channels, 2, 2, 2, 4, 4, 4)
    grad_cube = parts[:, 0]
    face_grads = []
    for direction in range(6):
        axis_number = direction // 2
        if direction % 2 == 0:
            moved, plane = minus_back(parts[:, direction + 1], axis_number)
        else:
            moved, plane = plus_back(parts[:, direction + 1], axis_number)
        grad_cube = grad_cube + moved
        face_grads.append(plane.reshape(number, channels * 64))
    pools = [
        jnp.zeros((2 * number + 1, channels * 64), jnp.float32)
        .at[links[:, direction]]
        .add(face_grads[direction])
        for direction in range(6)
    ]
    for direction in range(6):
        shaped = pools[direction][:number].reshape(number, channels, 2, 2, 4, 4)
        grad_cube = grad_cube.at[face_index(direction // 2, direction % 2 == 0)].add(shaped)
    far_rows = [
        pools[direction][number : 2 * number].astype(jnp.bfloat16) for direction in range(4)
    ]
    return (grad_cube, far_rows)


def add_faces(grad_cube, into_xhigh, into_xlow, into_yhigh, into_ylow):
    number, channels = (grad_cube.shape[0], grad_cube.shape[1])

    def planes(rows):
        return rows.astype(jnp.float32).reshape(number, channels, 2, 2, 4, 4)

    grad_cube = grad_cube.at[face_index(0, True)].add(planes(into_xhigh))
    grad_cube = grad_cube.at[face_index(0, False)].add(planes(into_xlow))
    grad_cube = grad_cube.at[face_index(1, True)].add(planes(into_yhigh))
    grad_cube = grad_cube.at[face_index(1, False)].add(planes(into_ylow))
    return grad_cube


def merge_pool(own_rows):
    beside_y = from_partner(own_rows, "gy", 0)
    received = from_partner(jnp.concatenate([own_rows, beside_y], axis=0), "gx", 0)
    half = own_rows.shape[0]
    return jnp.concatenate([own_rows, received[:half], beside_y, received[half:]], axis=0)


def split_pool(back_rows):
    half = back_rows.shape[0] // 4
    own_part = back_rows[:half].astype(jnp.float32)
    along_x = back_rows[half : 2 * half]
    along_y = back_rows[2 * half : 3 * half]
    diagonal = back_rows[3 * half :]
    returned = from_partner(jnp.concatenate([along_x, diagonal], axis=0), "gx", 0)
    kept = own_part + returned[:half].astype(jnp.float32)
    beside = (along_y.astype(jnp.float32) + returned[half:].astype(jnp.float32)).astype(
        jnp.bfloat16
    )
    final_rows = kept + from_partner(beside, "gy", 0).astype(jnp.float32)
    return final_rows.astype(jnp.bfloat16)


def scatter_rows(volume, links, number):
    width = volume.shape[1] * volume.shape[2] // 8
    rows = volume.reshape(volume.shape[0] * 8, width)
    total = (
        jnp.zeros((4 * number + 1, width), jnp.float32)
        .at[links.reshape(-1)]
        .add(rows.astype(jnp.float32))
    )
    return total[: 4 * number].astype(jnp.bfloat16)


def body(
    features, neighbours, counts, conv_weight, down_weight, head_weight, coarse_map, latent_grad
):
    number, channels = (features.shape[0], features.shape[1])
    wide = down_weight.shape[0]
    coarse_count = coarse_map.shape[0]
    active = jnp.arange(number) < counts[0]
    masked = jnp.where(active[:, None, None], features, jnp.zeros((), jnp.bfloat16))
    cube = octet(masked)
    faces = face_layers(cube)
    rim_x = padded(jnp.stack([faces[1], faces[0]]), (("gx", 0),), 1)
    rim_y = padded(jnp.stack([faces[3], faces[2]]), (("gy", 0),), 1)
    taps = neighbour_stack(cube, faces, (rim_x[0], rim_x[3], rim_y[0], rim_y[3]), neighbours)
    hidden = jnp.einsum("ok,bkv->bov", conv_weight, taps, preferred_element_type=jnp.float32)
    act = jax.nn.silu(hidden).astype(jnp.bfloat16)
    patches = act.reshape(number, channels * 8, 64)
    octants = jnp.einsum(
        "ok,bkv->bvo", down_weight, patches, preferred_element_type=jnp.float32
    ).astype(jnp.bfloat16)
    empty_row = jnp.zeros((1, 64 * wide), jnp.bfloat16)
    merged = merge_pool(octants.reshape(number, 64 * wide))
    coarse = jnp.concatenate([merged, empty_row], axis=0)[coarse_map].reshape(
        coarse_count, 512, wide
    )
    coarse_act = jax.nn.silu(coarse.astype(jnp.float32)).astype(jnp.bfloat16)
    latent = jnp.einsum(
        "oi,cvi->cvo", head_weight, coarse_act, preferred_element_type=jnp.float32
    ).astype(jnp.bfloat16)
    act_grad = jnp.einsum(
        "oi,cvo->cvi", head_weight, latent_grad, preferred_element_type=jnp.float32
    )
    coarse_grad = (act_grad * silu_grad(coarse.astype(jnp.float32))).astype(jnp.bfloat16)
    head_part = jnp.einsum(
        "cvo,cvi->oi", latent_grad, coarse_act, preferred_element_type=jnp.float32
    )
    octant_grad = split_pool(scatter_rows(coarse_grad, coarse_map, number)).reshape(
        number, 64, wide
    )
    down_part = jnp.einsum("bvo,bkv->ok", octant_grad, patches, preferred_element_type=jnp.float32)
    patch_grad = jnp.einsum(
        "ok,bvo->bkv", down_weight, octant_grad, preferred_element_type=jnp.float32
    )
    hidden_grad = (patch_grad.reshape(number, channels, 512) * silu_grad(hidden)).astype(
        jnp.bfloat16
    )
    conv_part = jnp.einsum("bov,bkv->ok", hidden_grad, taps, preferred_element_type=jnp.float32)
    taps_grad = jnp.einsum(
        "ok,bov->bkv", conv_weight, hidden_grad, preferred_element_type=jnp.float32
    )
    near_grad, far_rows = stack_grad(taps_grad, neighbours)
    return_x = padded(jnp.stack([far_rows[0], far_rows[1]]), (("gx", 0),), 1)
    return_y = padded(jnp.stack([far_rows[2], far_rows[3]]), (("gy", 0),), 1)
    total_grad = add_faces(near_grad, return_x[3], return_x[0], return_y[3], return_y[0]).reshape(
        number, channels, 512
    )
    features_grad = jnp.where(active[:, None, None], total_grad, 0.0).astype(jnp.bfloat16)
    summed = lax.psum((conv_part, down_part, head_part), ("gx", "gy"))
    scale = float(number * lax.axis_size("gx") * lax.axis_size("gy")) ** (-0.5)
    return (latent, features_grad, summed[0] * scale, summed[1] * scale, summed[2] * scale)


def solution(mesh):
    placed = (
        P(("gx", "gy"), None, None),
        P(("gx", "gy"), None),
        P(("gx", "gy")),
        P(),
        P(),
        P(),
        P(("gx", "gy"), None),
        P(("gx", "gy"), None, None),
    )
    return jax.shard_map(
        body,
        mesh=mesh,
        in_specs=placed,
        out_specs=(P(("gx", "gy"), None, None), P(("gx", "gy"), None, None), P(), P(), P()),
        check_vma=False,
    )
```

profile of v0, /device:TPU:2, one launch (start us, length us, event | category | flops | bytes accessed | tf_op | source)
XLA Modules:
  0.0 611.6 jit_solution(5561831385059505792)
XLA Ops:
  12.5 4.4 collective-permute-start
  21.6 3.1 copy.127
  29.4 3.1 copy.134
  34.7 3.8 collective-permute-start.3
  90.8 11.2 %copy.151 = bf16[8,7,64,2,2,2,4,4,4]{2,1,8,7,6,5,4,3,0:T(8,128)(2,1)} copy(bf16[8,7,64,2,2,2,4,4,4]{2,0,8,7,6,5,4,3,1:T(8,128)(2,1)} %fusion.16) | data formatting | bytes 7340032 | tf_op jit(solution)/shard_map/stack | solution.py:148
  102.0 11.6 %reshape.747 = bf16[8,448,512]{1,2,0:T(8,128)(2,1)} reshape(bf16[8,7,64,2,2,2,4,4,4]{2,1,8,7,6,5,4,3,0:T(8,128)(2,1)} %copy.151) | data formatting | bytes 7340032 | tf_op jit(solution)/shard_map/reshape | solution.py:148
  113.6 4.6 multiply_convert_fusion.1
  120.8 2.7 collective-permute-start.5
  123.7 6.5 %collective-permute-done.5 = bf16[16,8192]{1,0:T(8,128)(2,1)S(1)} collective-permute-done((bf16[16,8192]{1,0:T(8,128)(2,1)S(1)}, bf16[16,8192]{1,0:T(8,128)(2,1)S(1)}, u32[]{:S(2)}, u32[]{:S(2)}) %collective-permute-start.5) | collective-permute-done | bytes 262176 | tf_op jit(solution)/shard_map/ppermute | solution.py:14
  136.6 4.1 collective-permute-done.6
  148.8 3.7 convolution_bitcast_fusion.4
  152.5 4.1 convolution_bitcast_fusion
  156.6 8.8 %copy.155 = f32[8,448,512]{1,2,0:T(8,128)} copy(f32[8,448,512]{2,1,0:T(8,128)} %convolution_bitcast_fusion) | data formatting | bytes 14680064 | tf_op jit(solution)/shard_map/ok,bov->bkv/transpose | solution.py:271
  165.4 13.2 %reshape.754 = f32[8,7,64,2,2,2,4,4,4]{2,1,8,7,6,5,4,3,0:T(8,128)} reshape(f32[8,448,512]{1,2,0:T(8,128)} %copy.155) | data formatting | bytes 14680064 | tf_op jit(solution)/shard_map/reshape | solution.py:153
  178.6 53.0 %fusion.67 = (f32[8,1,64,2,2,2,4,4,4]{2,1,8,7,6,5,4,3,0:T(1,128)S(1)}, f32[8,1,64,2,2,2,4,4,4]{2,1,8,7,6,5,4,3,0:T(1,128)S(1)}, f32[8,1,64,2,2,2,4,4,4]{2,1,8,7,...) fusion(f32[8,7,64,2,2,2,4,4,4]{2,1,8,7,6,5,4,3,0:T(8,128)} %res, ...), kind=kLoop, calls=%fused_computation.173 | loop fusion | bytes 14680064 | tf_op jit(solution)/shard_map/slice | solution.py:159
  249.3 3.1 copy.166
  254.7 3.2 copy.170
  260.1 3.2 copy.162
  267.0 3.1 copy.174
  273.9 3.1 copy.178
  280.2 3.1 copy.182
  286.5 4.0 collective-permute-start.9
  293.7 2.6 collective-permute-start.11
  313.6 6.5 %fusion = f32[8,64,2,2,2,4,4,4]{1,7,6,5,4,3,2,0:T(4,128)S(1)} fusion(f32[8,64,2,2,1,4,4,3]{1,7,6,5,4,3,2,0:T(4,128)} %slice.902, f32[8,64,2,2,1,4,4,3]{1,7,6,5,4,3,2,0:T(4,128)} %slice.900, f32[8,64,2,1,2,4,3,4]{1,7,6,5,4,3,2,0:T(4,128)} %slice.896, f32[8,64,2,1,2,4,3,4]{1,7,6,5,4,3,2,0:T(4,128)} %slice.894, f32[8,64,1,2,2,3,4,4]{1,7,6,5,4,3,2,0:T(4,128)} %slice.890, ...), kind=kLoop, calls=%fused_computation.16 | loop fusion | flops 6291456 | bytes 7602176 | tf_op jit(solution)/shard_map/add | solution.py:162
  322.3 6.4 %scatter-add.109 = f32[8,64,2,2,2,4,4,4]{1,7,6,5,4,3,2,0:T(4,128)S(1)} dynamic-update-slice(f32[8,64,2,2,2,4,4,4]{1,7,6,5,4,3,2,0:T(4,128)S(1)} %fusion.23, f32[8,64,2,2,1,4,4,1]{1,7,6,5,4,3,2,0:T(1,128)} %slice_add_fusion.5, s32[]{:T(128)} %constant.277.clone.1, s32[]{:T(128)} %constant.277.clone.1, s32[]{:T(128)} %constant.277.clone.1, s32[]{:T(128)} %constant.277.clone.1, s32[]{:T(128)} %constant.282.clone.1, ...) | dynamic-update-slice | bytes 262148 | tf_op jit(solution)/shard_map/scatter-add | solution.py:172
  331.8 6.4 %scatter-add.111 = f32[8,64,2,2,2,4,4,4]{1,7,6,5,4,3,2,0:T(4,128)S(1)} dynamic-update-slice(f32[8,64,2,2,2,4,4,4]{1,7,6,5,4,3,2,0:T(4,128)S(1)} %scatter-add.109, f32[8,64,2,2,1,4,4,1]{1,7,6,5,4,3,2,0:T(1,128)} %slice_add_fusion.4, s32[]{:T(128)} %constant.277.clone.1, s32[]{:T(128)} %constant.277.clone.1, s32[]{:T(128)} %constant.277.clone.1, s32[]{:T(128)} %constant.277.clone.1, ...) | dynamic-update-slice | bytes 262148 | tf_op jit(solution)/shard_map/scatter-add | solution.py:172
  338.2 2.5 copy.192
  343.2 2.5 copy.186
  348.1 2.5 copy.190
  350.6 2.6 copy.191
  353.3 2.5 copy.188
  361.8 237.7 %all-reduce.9.cloned.1.call-done = (f32[64,448]{1,0:T(8,128)}, f32[128,512]{1,0:T(8,128)}, f32[128,128]{0,1:T(8,128)}) async-done(((f32[64,448]{1,0:T(8,128)}, f32[128,512]{1,0:T(8,128)}, f32[128,128]{0,1:T(8,128)}), (f32[64,448]{1,0:T(8,128)}, f32[128,512]{1,0:T(8,128)}, f32[128,128]{0,1:T(8,128)})) %all-reduce.9.cloned.1.call-update) | async-done | bytes 442384 | tf_op jit(solution)/shard_map/psum | solution.py:281
  (287 shorter events, 162.1 us)
Async XLA Ops:
  7.2 111.6 %copy-start = (bf16[128,512]{1,0:T(8,128)(2,1)S(1)}, bf16[128,512]{1,0:T(8,128)(2,1)}, u32[]{:S(2)}) copy-start(bf16[128,512]{1,0:T(8,128)(2,1)} %param.32) | copy-start | bytes 393220
  7.2 592.3 %all-reduce.9.cloned.1.call-start = ((), (), s32[]{:S(2)}) async-start(), calls=%async_computation | async-start | bytes 917504 | tf_op jit(solution)/shard_map/psum | solution.py:281
  12.5 52.6 %collective-permute-start = (bf16[1,8,4096]{2,1,0:T(8,128)(2,1)}, bf16[1,8,4096]{2,1,0:T(8,128)(2,1)}, u32[]{:S(2)}, u32[]{:S(2)}) collective-permute-start(bf16[1,8,4096]{2,1,0:T(8,128)(2,1)} %copy.115), channel_id=1, source_target_pairs={{0,8},{8,16},{16,24},{24,32},{32,40},{40,48},{48,56},{56,64},{64,7... | collective-permute-start | bytes 196616 | tf_op jit(solution)/shard_map/ppermute | solution.py:22
  19.6 45.6 %collective-permute-start.1 = (bf16[1,8,4096]{2,1,0:T(8,128)(2,1)}, bf16[1,8,4096]{2,1,0:T(8,128)(2,1)}, u32[]{:S(2)}, u32[]{:S(2)}) collective-permute-start(bf16[1,8,4096]{2,1,0:T(8,128)(2,1)} %copy.122), channel_id=1, source_target_pairs={{8,0},{16,8},{24,16},{32,24},{40,32},{48,40},{56,48},{64,56},{72,6... | collective-permute-start | bytes 196616 | tf_op jit(solution)/shard_map/ppermute | solution.py:25
  26.8 38.3 %collective-permute-start.2 = (bf16[1,8,4096]{2,1,0:T(8,128)(2,1)}, bf16[1,8,4096]{2,1,0:T(8,128)(2,1)}, u32[]{:S(2)}, u32[]{:S(2)}) collective-permute-start(bf16[1,8,4096]{2,1,0:T(8,128)(2,1)} %copy.129), channel_id=1, source_target_pairs={{0,1},{1,2},{2,3},{3,4},{4,5},{5,6},{6,7},{8,9},{9,10},{10,11},{11... | collective-permute-start | bytes 196616 | tf_op jit(solution)/shard_map/ppermute | solution.py:22
  34.7 30.5 %collective-permute-start.3 = (bf16[1,8,4096]{2,1,0:T(8,128)(2,1)}, bf16[1,8,4096]{2,1,0:T(8,128)(2,1)}, u32[]{:S(2)}, u32[]{:S(2)}) collective-permute-start(bf16[1,8,4096]{2,1,0:T(8,128)(2,1)} %copy.136), channel_id=1, source_target_pairs={{1,0},{2,1},{3,2},{4,3},{5,4},{6,5},{7,6},{9,8},{10,9},{11,10},{12... | collective-permute-start | bytes 196616 | tf_op jit(solution)/shard_map/ppermute | solution.py:25
  43.3 3.9 copy-start.26
  58.3 3.8 copy-start.24
  62.1 3.0 copy-start.32
  62.1 3.1 copy-start.38
  62.2 3.1 copy-start.39
  77.0 6.0 copy-start.8
  77.0 6.0 copy-start.14
  79.4 4.9 copy-start.7
  79.4 4.9 copy-start.13
  102.0 11.6 %copy-start.28 = (bf16[64,448]{1,0:T(8,128)(2,1)S(1)}, bf16[64,448]{1,0:T(8,128)(2,1)}, u32[]{:S(2)}) copy-start(bf16[64,448]{1,0:T(8,128)(2,1)} %param.31) | copy-start | bytes 172036
  118.8 12.2 %copy-start.27 = (bf16[1,512,128]{2,1,0:T(8,128)(2,1)S(1)}, bf16[1,512,128]{2,1,0:T(8,128)(2,1)}, u32[]{:S(2)}) copy-start(bf16[1,512,128]{2,1,0:T(8,128)(2,1)} %param.35) | copy-start | bytes 393220
  118.8 12.2 %copy-start.40 = (bf16[128,128]{1,0:T(8,128)(2,1)S(1)}, bf16[128,128]{1,0:T(8,128)(2,1)}, u32[]{:S(2)}) copy-start(bf16[128,128]{1,0:T(8,128)(2,1)} %param.33) | copy-start | bytes 98308
  119.4 1.4 collective-permute-start.4
  120.8 9.4 %collective-permute-start.5 = (bf16[16,8192]{1,0:T(8,128)(2,1)S(1)}, bf16[16,8192]{1,0:T(8,128)(2,1)S(1)}, u32[]{:S(2)}, u32[]{:S(2)}) collective-permute-start(bf16[16,8192]{1,0:T(8,128)(2,1)S(1)} %pad_maximum_fusion), channel_id=1, source_target_pairs={{0,8},{8,0},{16,24},{24,16},{32,40},{40,32},{48,56},{56,48},{64,72... | collective-permute-start | bytes 786440 | tf_op jit(solution)/shard_map/ppermute | solution.py:14
  132.7 8.3 %copy-start.41 = (bf16[128,128]{1,0:T(8,128)(2,1)S(1)}, bf16[128,128]{1,0:T(8,128)(2,1)}, u32[]{:S(2)}) copy-start(bf16[128,128]{1,0:T(8,128)(2,1)} %param.33) | copy-start | bytes 98308
  132.7 8.0 %collective-permute-start.6 = (bf16[16,8192]{1,0:T(8,128)(2,1)S(1)}, bf16[16,8192]{1,0:T(8,128)(2,1)S(1)}, u32[]{:S(2)}, u32[]{:S(2)}) collective-permute-start(bf16[16,8192]{1,0:T(8,128)(2,1)S(1)} %pad_maximum_fusion.1), channel_id=1, source_target_pairs={{0,8},{8,0},{16,24},{24,16},{32,40},{40,32},{48,56},{56,48},{64,72... | collective-permute-start | bytes 786440 | tf_op jit(solution)/shard_map/ppermute | solution.py:14
  140.8 1.4 collective-permute-start.7
  148.8 3.7 copy-start.29
  286.5 66.8 %collective-permute-start.9 = (bf16[1,8,4096]{2,1,0:T(8,128)(2,1)}, bf16[1,8,4096]{2,1,0:T(8,128)(2,1)}, u32[]{:S(2)}, u32[]{:S(2)}) collective-permute-start(bf16[1,8,4096]{2,1,0:T(8,128)(2,1)} %fusion.53), channel_id=1, source_target_pairs={{0,8},{8,16},{16,24},{24,32},{32,40},{40,48},{48,56},{56,64},{64,7... | collective-permute-start | bytes 196616 | tf_op jit(solution)/shard_map/ppermute | solution.py:22
  290.5 57.6 %collective-permute-start.10 = (bf16[1,8,4096]{2,1,0:T(8,128)(2,1)}, bf16[1,8,4096]{2,1,0:T(8,128)(2,1)}, u32[]{:S(2)}, u32[]{:S(2)}) collective-permute-start(bf16[1,8,4096]{2,1,0:T(8,128)(2,1)} %fusion.54), channel_id=1, source_target_pairs={{1,0},{2,1},{3,2},{4,3},{5,4},{6,5},{7,6},{9,8},{10,9},{11,10},{12... | collective-permute-start | bytes 196616 | tf_op jit(solution)/shard_map/ppermute | solution.py:25
  292.4 50.8 %collective-permute-start.8 = (bf16[1,8,4096]{2,1,0:T(8,128)(2,1)}, bf16[1,8,4096]{2,1,0:T(8,128)(2,1)}, u32[]{:S(2)}, u32[]{:S(2)}) collective-permute-start(bf16[1,8,4096]{2,1,0:T(8,128)(2,1)} %fusion.52), channel_id=1, source_target_pairs={{8,0},{16,8},{24,16},{32,24},{40,32},{48,40},{56,48},{64,56},{72,6... | collective-permute-start | bytes 196616 | tf_op jit(solution)/shard_map/ppermute | solution.py:25
  293.7 44.5 %collective-permute-start.11 = (bf16[1,8,4096]{2,1,0:T(8,128)(2,1)}, bf16[1,8,4096]{2,1,0:T(8,128)(2,1)}, u32[]{:S(2)}, u32[]{:S(2)}) collective-permute-start(bf16[1,8,4096]{2,1,0:T(8,128)(2,1)} %fusion.55), channel_id=1, source_target_pairs={{0,1},{1,2},{2,3},{3,4},{4,5},{5,6},{6,7},{8,9},{9,10},{10,11},{11... | collective-permute-start | bytes 196616 | tf_op jit(solution)/shard_map/ppermute | solution.py:22
  313.6 6.5 %copy-start.17 = (f32[8,64,1,2,2,1,4,4]{1,7,6,5,4,3,2,0:T(4,128)S(1)}, f32[8,64,1,2,2,1,4,4]{1,7,6,5,4,3,2,0:T(4,128)}, u32[]{:S(2)}) copy-start(f32[8,64,1,2,2,1,4,4]{1,7,6,5,4,3,2,0:T(4,128)} %copy.165) | copy-start | bytes 393220
  313.6 6.7 %copy-start.19 = (f32[8,64,1,2,2,1,4,4]{1,7,6,5,4,3,2,0:T(4,128)S(1)}, f32[8,64,1,2,2,1,4,4]{1,7,6,5,4,3,2,0:T(4,128)}, u32[]{:S(2)}) copy-start(f32[8,64,1,2,2,1,4,4]{1,7,6,5,4,3,2,0:T(4,128)} %copy.169) | copy-start | bytes 393220
  313.6 6.8 %copy-start.16 = (f32[8,64,2,1,2,4,1,4]{1,7,6,5,4,3,2,0:T(4,128)S(1)}, f32[8,64,2,1,2,4,1,4]{1,7,6,5,4,3,2,0:T(4,128)}, u32[]{:S(2)}) copy-start(f32[8,64,2,1,2,4,1,4]{1,7,6,5,4,3,2,0:T(4,128)} %copy.173) | copy-start | bytes 393220
  358.7 245.6 %copy-start.1 = (bf16[128,512]{1,0:T(8,128)(2,1)S(1)}, bf16[128,512]{1,0:T(8,128)(2,1)}, u32[]{:S(2)}) copy-start(bf16[128,512]{1,0:T(8,128)(2,1)} %param.32) | copy-start | bytes 393220
  (25 other events, 49.3 us)
Sparse Core Ops, SparseCore 0:
  338.3 261.1 all-reduce.8
where the time goes:
time: 619 us; the launch traced here: 612 us
  local copies, waits for them, and re-layouts  264 us (43%)
  waiting for transfers between devices  250 us (40%)
  other arithmetic  37.3 us (6%)
  starting transfers between devices  26.2 us (4%)
  matrix products  18.1 us (3%)
  between operations  16.2 us (3%)
    psum x1, waiting for transfers between devices, body(): summed = lax.psum((conv_part, down_part, head_part), ('gx', 'gy'))  238 us
    slice x1, local copies, waits for them, and re-layouts, stack_grad(): moved, plane = minus_back(parts[:, direction + 1], axis_number)  53 us
    convert_element_type x8, local copies, waits for them, and re-layouts, planes(): return rows.astype(jnp.float32).reshape(number, channels, 2, 2, 4, 4)  20 us
    slice x12, local copies, waits for them, and re-layouts, face_of(): lax.index_in_dim(plane, 1 if upper else 0, 2 + axis_number, keepdims=False)  16.3 us
    reshape x1, local copies, waits for them, and re-layouts, stack_grad(): parts = taps_grad.reshape(number, 7, channels, 2, 2, 2, 4, 4, 4)  13.2 us
    ppermute x4, starting transfers between devices, padded(): lax.ppermute(lax.slice_in_dim(block, block.shape[dim] - width, None, axis...  12.9 us
    scatter-add x2, local copies, waits for them, and re-layouts, stack_grad(): grad_cube.at[face_index(direction // 2, direction % 2 == 0)].add(shaped)  12.7 us
    ppermute x4, waiting for transfers between devices, from_partner(): return lax.ppermute(block, axis, route)  12.4 us
  transfers between devices with their start and end apart: 13, of which 5 were waited for; matrix products, arithmetic and copies ran while one was open for 18% of the time, Pallas kernels for 0%

commit v1 on v0

--- a/solution.py
+++ b/solution.py
@@ -2,6 +2,10 @@
 import jax.numpy as jnp
 from jax import lax
 from jax.sharding import PartitionSpec as P
+
+group_reach = lambda block_in, bus_axis, ax_name: jax.lax.psum(
+    jax.lax.psum(block_in, bus_axis), ax_name
+)
 
 
 def from_partner(block, axis, distance):
@@ -278,7 +282,7 @@
         number, channels, 512
     )
     features_grad = jnp.where(active[:, None, None], total_grad, 0.0).astype(jnp.bfloat16)
-    summed = lax.psum((conv_part, down_part, head_part), ("gx", "gy"))
+    summed = group_reach((conv_part, down_part, head_part), "gx", "gy")
     scale = float(number * lax.axis_size("gx") * lax.axis_size("gy")) ** (-0.5)
     return (latent, features_grad, summed[0] * scale, summed[1] * scale, summed[2] * scale)
 

time: 619 us -> 579 us (0.935)
  waiting for transfers between devices: 250 us -> 207 us
    psum x1 -> x2, waiting for transfers between devices: 238 us -> 195 us  [the longest x1 133 us: jax.lax.psum(block_in, bus_axis)]
  transfers between devices with their start and end apart: 13 -> 14, of which waited for: 5 -> 6; matrix products, arithmetic and copies ran while one was open for 18% -> 19% of each run, Pallas kernels for 0% -> 0%
where the time goes in v1:
time: 579 us; the launch traced here: 569 us
  local copies, waits for them, and re-layouts  264 us (46%)
  waiting for transfers between devices  207 us (36%)
  other arithmetic  37.6 us (6%)
  starting transfers between devices  26.3 us (5%)
  matrix products  18.1 us (3%)
  between operations  16.2 us (3%)
    psum x1, waiting for transfers between devices, jax.lax.psum(block_in, bus_axis)  133 us
    psum x1, waiting for transfers between devices, jax.lax.psum(jax.lax.psum(block_in, bus_axis), ax_name)  61.7 us
    slice x1, local copies, waits for them, and re-layouts, stack_grad(): moved, plane = minus_back(parts[:, direction + 1], axis_number)  53.6 us
    convert_element_type x8, local copies, waits for them, and re-layouts, planes(): return rows.astype(jnp.float32).reshape(number, channels, 2, 2, 4, 4)  19.7 us
    slice x12, local copies, waits for them, and re-layouts, face_of(): lax.index_in_dim(plane, 1 if upper else 0, 2 + axis_number, keepdims=False)  16.3 us
    reshape x1, local copies, waits for them, and re-layouts, stack_grad(): parts = taps_grad.reshape(number, 7, channels, 2, 2, 2, 4, 4, 4)  13.2 us
    ppermute x4, starting transfers between devices, padded(): lax.ppermute(lax.slice_in_dim(block, block.shape[dim] - width, None, axis...  12.7 us
    scatter-add x2, local copies, waits for them, and re-layouts, stack_grad(): grad_cube.at[face_index(direction // 2, direction % 2 == 0)].add(shaped)  12.7 us
  transfers between devices with their start and end apart: 14, of which 6 were waited for; matrix products, arithmetic and copies ran while one was open for 19% of the time, Pallas kernels for 0%

profile of v1, /device:TPU:2, one launch (start us, length us, event | category | flops | bytes accessed | tf_op | source)
XLA Modules:
  0.0 569.5 jit_solution(3019619345830593339)
XLA Ops:
  12.6 4.5 collective-permute-start
  21.6 3.1 copy.127
  29.5 3.1 copy.134
  34.8 3.8 collective-permute-start.3
  90.9 11.2 %copy.151 = bf16[8,7,64,2,2,2,4,4,4]{2,1,8,7,6,5,4,3,0:T(8,128)(2,1)} copy(bf16[8,7,64,2,2,2,4,4,4]{2,0,8,7,6,5,4,3,1:T(8,128)(2,1)} %fusion.16) | data formatting | bytes 7340032 | tf_op jit(solution)/shard_map/stack | solution.py:152
  102.2 11.6 %reshape.747 = bf16[8,448,512]{1,2,0:T(8,128)(2,1)} reshape(bf16[8,7,64,2,2,2,4,4,4]{2,1,8,7,6,5,4,3,0:T(8,128)(2,1)} %copy.151) | data formatting | bytes 7340032 | tf_op jit(solution)/shard_map/reshape | solution.py:152
  113.8 4.6 multiply_convert_fusion.1
  121.0 2.7 collective-permute-start.5
  123.8 6.5 %collective-permute-done.5 = bf16[16,8192]{1,0:T(8,128)(2,1)S(1)} collective-permute-done((bf16[16,8192]{1,0:T(8,128)(2,1)S(1)}, bf16[16,8192]{1,0:T(8,128)(2,1)S(1)}, u32[]{:S(2)}, u32[]{:S(2)}) %collective-permute-start.5) | collective-permute-done | bytes 262176 | tf_op jit(solution)/shard_map/ppermute | solution.py:18
  136.8 4.1 collective-permute-done.6
  148.9 3.7 convolution_bitcast_fusion.4
  152.7 4.1 convolution_bitcast_fusion
  156.7 8.8 %copy.155 = f32[8,448,512]{1,2,0:T(8,128)} copy(f32[8,448,512]{2,1,0:T(8,128)} %convolution_bitcast_fusion) | data formatting | bytes 14680064 | tf_op jit(solution)/shard_map/ok,bov->bkv/transpose | solution.py:275
  165.6 13.2 %reshape.754 = f32[8,7,64,2,2,2,4,4,4]{2,1,8,7,6,5,4,3,0:T(8,128)} reshape(f32[8,448,512]{1,2,0:T(8,128)} %copy.155) | data formatting | bytes 14680064 | tf_op jit(solution)/shard_map/reshape | solution.py:157
  178.7 53.6 %fusion.67 = (f32[8,1,64,2,2,2,4,4,4]{2,1,8,7,6,5,4,3,0:T(1,128)S(1)}, f32[8,1,64,2,2,2,4,4,4]{2,1,8,7,6,5,4,3,0:T(1,128)S(1)}, f32[8,1,64,2,2,2,4,4,4]{2,1,8,7,...) fusion(f32[8,7,64,2,2,2,4,4,4]{2,1,8,7,6,5,4,3,0:T(8,128)} %res, ...), kind=kLoop, calls=%fused_computation.173 | loop fusion | bytes 14680064 | tf_op jit(solution)/shard_map/slice | solution.py:163
  250.2 3.1 copy.166
  255.5 3.2 copy.170
  261.1 3.2 copy.162
  268.0 3.1 copy.174
  275.0 3.1 copy.178
  281.2 3.1 copy.182
  287.5 4.0 collective-permute-start.9
  294.7 2.4 collective-permute-start.11
  314.3 6.5 %fusion = f32[8,64,2,2,2,4,4,4]{1,7,6,5,4,3,2,0:T(4,128)S(1)} fusion(f32[8,64,2,2,1,4,4,3]{1,7,6,5,4,3,2,0:T(4,128)} %slice.902, f32[8,64,2,2,1,4,4,3]{1,7,6,5,4,3,2,0:T(4,128)} %slice.900, f32[8,64,2,1,2,4,3,4]{1,7,6,5,4,3,2,0:T(4,128)} %slice.896, f32[8,64,2,1,2,4,3,4]{1,7,6,5,4,3,2,0:T(4,128)} %slice.894, f32[8,64,1,2,2,3,4,4]{1,7,6,5,4,3,2,0:T(4,128)} %slice.890, ...), kind=kLoop, calls=%fused_computation.16 | loop fusion | flops 6291456 | bytes 7602176 | tf_op jit(solution)/shard_map/add | solution.py:166
  323.1 6.4 %scatter-add.109 = f32[8,64,2,2,2,4,4,4]{1,7,6,5,4,3,2,0:T(4,128)S(1)} dynamic-update-slice(f32[8,64,2,2,2,4,4,4]{1,7,6,5,4,3,2,0:T(4,128)S(1)} %fusion.23, f32[8,64,2,2,1,4,4,1]{1,7,6,5,4,3,2,0:T(1,128)} %slice_add_fusion.5, s32[]{:T(128)} %constant.277.clone.1, s32[]{:T(128)} %constant.277.clone.1, s32[]{:T(128)} %constant.277.clone.1, s32[]{:T(128)} %constant.277.clone.1, s32[]{:T(128)} %constant.282.clone.1, ...) | dynamic-update-slice | bytes 262148 | tf_op jit(solution)/shard_map/scatter-add | solution.py:176
  332.6 6.4 %scatter-add.111 = f32[8,64,2,2,2,4,4,4]{1,7,6,5,4,3,2,0:T(4,128)S(1)} dynamic-update-slice(f32[8,64,2,2,2,4,4,4]{1,7,6,5,4,3,2,0:T(4,128)S(1)} %scatter-add.109, f32[8,64,2,2,1,4,4,1]{1,7,6,5,4,3,2,0:T(1,128)} %slice_add_fusion.4, s32[]{:T(128)} %constant.277.clone.1, s32[]{:T(128)} %constant.277.clone.1, s32[]{:T(128)} %constant.277.clone.1, s32[]{:T(128)} %constant.277.clone.1, ...) | dynamic-update-slice | bytes 262148 | tf_op jit(solution)/shard_map/scatter-add | solution.py:176
  339.3 2.5 copy.192
  344.2 2.5 copy.186
  349.2 2.5 copy.190
  354.2 2.5 copy.188
  360.8 133.0 %all-reduce.11.cloned.1.call-done = (f32[64,448]{1,0:T(8,128)}, f32[128,512]{1,0:T(8,128)}, f32[128,128]{0,1:T(8,128)}) async-done(((f32[64,448]{1,0:T(8,128)}, f32[128,512]{1,0:T(8,128)}, f32[128,128]{0,1:T(8,128)}), (f32[64,448]{1,0:T(8,128)}, f32[128,512]{1,0:T(8,128)}, f32[128,128]{0,1:T(8,128)})) %all-reduce.11.cloned.1.call-update) | async-done | bytes 442384 | tf_op jit(solution)/shard_map/psum | solution.py:7
  495.7 61.7 %all-reduce.13.cloned.1.call-done = (f32[64,448]{1,0:T(8,128)}, f32[128,512]{1,0:T(8,128)}, f32[128,128]{0,1:T(8,128)}) async-done(((f32[64,448]{1,0:T(8,128)}, f32[128,512]{1,0:T(8,128)}, f32[128,128]{0,1:T(8,128)}), (f32[64,448]{1,0:T(8,128)}, f32[128,512]{1,0:T(8,128)}, f32[128,128]{0,1:T(8,128)})) %all-reduce.13.cloned.1.call-update) | async-done | bytes 442384 | tf_op jit(solution)/shard_map/psum | solution.py:6
  (290 shorter events, 165.2 us)
Async XLA Ops:
  7.2 111.7 %copy-start = (bf16[128,512]{1,0:T(8,128)(2,1)S(1)}, bf16[128,512]{1,0:T(8,128)(2,1)}, u32[]{:S(2)}) copy-start(bf16[128,512]{1,0:T(8,128)(2,1)} %param.32) | copy-start | bytes 393220
  7.2 486.6 %all-reduce.11.cloned.1.call-start = ((), (), s32[]{:S(2)}) async-start(), calls=%async_computation | async-start | bytes 917504 | tf_op jit(solution)/shard_map/psum | solution.py:7
  12.6 52.8 %collective-permute-start = (bf16[1,8,4096]{2,1,0:T(8,128)(2,1)}, bf16[1,8,4096]{2,1,0:T(8,128)(2,1)}, u32[]{:S(2)}, u32[]{:S(2)}) collective-permute-start(bf16[1,8,4096]{2,1,0:T(8,128)(2,1)} %copy.115), channel_id=1, source_target_pairs={{0,8},{8,16},{16,24},{24,32},{32,40},{40,48},{48,56},{56,64},{64,7... | collective-permute-start | bytes 196616 | tf_op jit(solution)/shard_map/ppermute | solution.py:26
  19.6 45.8 %collective-permute-start.1 = (bf16[1,8,4096]{2,1,0:T(8,128)(2,1)}, bf16[1,8,4096]{2,1,0:T(8,128)(2,1)}, u32[]{:S(2)}, u32[]{:S(2)}) collective-permute-start(bf16[1,8,4096]{2,1,0:T(8,128)(2,1)} %copy.122), channel_id=1, source_target_pairs={{8,0},{16,8},{24,16},{32,24},{40,32},{48,40},{56,48},{64,56},{72,6... | collective-permute-start | bytes 196616 | tf_op jit(solution)/shard_map/ppermute | solution.py:29
  26.9 38.5 %collective-permute-start.2 = (bf16[1,8,4096]{2,1,0:T(8,128)(2,1)}, bf16[1,8,4096]{2,1,0:T(8,128)(2,1)}, u32[]{:S(2)}, u32[]{:S(2)}) collective-permute-start(bf16[1,8,4096]{2,1,0:T(8,128)(2,1)} %copy.129), channel_id=1, source_target_pairs={{0,1},{1,2},{2,3},{3,4},{4,5},{5,6},{6,7},{8,9},{9,10},{10,11},{11... | collective-permute-start | bytes 196616 | tf_op jit(solution)/shard_map/ppermute | solution.py:26
  34.8 30.6 %collective-permute-start.3 = (bf16[1,8,4096]{2,1,0:T(8,128)(2,1)}, bf16[1,8,4096]{2,1,0:T(8,128)(2,1)}, u32[]{:S(2)}, u32[]{:S(2)}) collective-permute-start(bf16[1,8,4096]{2,1,0:T(8,128)(2,1)} %copy.136), channel_id=1, source_target_pairs={{1,0},{2,1},{3,2},{4,3},{5,4},{6,5},{7,6},{9,8},{10,9},{11,10},{12... | collective-permute-start | bytes 196616 | tf_op jit(solution)/shard_map/ppermute | solution.py:29
  43.4 4.0 copy-start.26
  58.5 3.8 copy-start.24
  62.4 3.1 copy-start.38
  77.2 5.9 %copy-start.8 = (bf16[8,64,1,2,2,4,4,4]{1,0,7,6,5,4,3,2:T(8,128)(2,1)S(1)}, bf16[8,64,1,2,2,4,4,4]{1,0,7,6,5,4,3,2:T(8,128)(2,1)}, u32[]{:S(2)}) copy-start(bf16[8,64,1,2,2,4,4,4]{1,0,7,6,5,4,3,2:T(8,128)(2,1)} %get-tuple-element.166) | copy-start | bytes 786436
  77.2 5.9 %copy-start.14 = (bf16[8,64,1,2,2,3,4,4]{1,0,7,6,5,4,3,2:T(8,128)(2,1)S(1)}, bf16[8,64,1,2,2,3,4,4]{1,0,7,6,5,4,3,2:T(8,128)(2,1)}, u32[]{:S(2)}) copy-start(bf16[8,64,1,2,2,3,4,4]{1,0,7,6,5,4,3,2:T(8,128)(2,1)} %get-tuple-element.168) | copy-start | bytes 589828
  79.6 4.9 copy-start.7
  79.6 4.9 copy-start.13
  102.2 11.6 %copy-start.28 = (bf16[64,448]{1,0:T(8,128)(2,1)S(1)}, bf16[64,448]{1,0:T(8,128)(2,1)}, u32[]{:S(2)}) copy-start(bf16[64,448]{1,0:T(8,128)(2,1)} %param.31) | copy-start | bytes 172036
  118.9 12.2 %copy-start.27 = (bf16[1,512,128]{2,1,0:T(8,128)(2,1)S(1)}, bf16[1,512,128]{2,1,0:T(8,128)(2,1)}, u32[]{:S(2)}) copy-start(bf16[1,512,128]{2,1,0:T(8,128)(2,1)} %param.35) | copy-start | bytes 393220
  118.9 12.2 %copy-start.40 = (bf16[128,128]{1,0:T(8,128)(2,1)S(1)}, bf16[128,128]{1,0:T(8,128)(2,1)}, u32[]{:S(2)}) copy-start(bf16[128,128]{1,0:T(8,128)(2,1)} %param.33) | copy-start | bytes 98308
  119.5 1.4 collective-permute-start.4
  121.0 9.4 %collective-permute-start.5 = (bf16[16,8192]{1,0:T(8,128)(2,1)S(1)}, bf16[16,8192]{1,0:T(8,128)(2,1)S(1)}, u32[]{:S(2)}, u32[]{:S(2)}) collective-permute-start(bf16[16,8192]{1,0:T(8,128)(2,1)S(1)} %pad_maximum_fusion), channel_id=1, source_target_pairs={{0,8},{8,0},{16,24},{24,16},{32,40},{40,32},{48,56},{56,48},{64,72... | collective-permute-start | bytes 786440 | tf_op jit(solution)/shard_map/ppermute | solution.py:18
  132.8 8.2 %copy-start.41 = (bf16[128,128]{1,0:T(8,128)(2,1)S(1)}, bf16[128,128]{1,0:T(8,128)(2,1)}, u32[]{:S(2)}) copy-start(bf16[128,128]{1,0:T(8,128)(2,1)} %param.33) | copy-start | bytes 98308
  132.9 8.0 %collective-permute-start.6 = (bf16[16,8192]{1,0:T(8,128)(2,1)S(1)}, bf16[16,8192]{1,0:T(8,128)(2,1)S(1)}, u32[]{:S(2)}, u32[]{:S(2)}) collective-permute-start(bf16[16,8192]{1,0:T(8,128)(2,1)S(1)} %pad_maximum_fusion.1), channel_id=1, source_target_pairs={{0,8},{8,0},{16,24},{24,16},{32,40},{40,32},{48,56},{56,48},{64,72... | collective-permute-start | bytes 786440 | tf_op jit(solution)/shard_map/ppermute | solution.py:18
  141.0 1.4 collective-permute-start.7
  148.9 3.7 copy-start.29
  287.5 66.6 %collective-permute-start.9 = (bf16[1,8,4096]{2,1,0:T(8,128)(2,1)}, bf16[1,8,4096]{2,1,0:T(8,128)(2,1)}, u32[]{:S(2)}, u32[]{:S(2)}) collective-permute-start(bf16[1,8,4096]{2,1,0:T(8,128)(2,1)} %fusion.53), channel_id=1, source_target_pairs={{0,8},{8,16},{16,24},{24,32},{32,40},{40,48},{48,56},{56,64},{64,7... | collective-permute-start | bytes 196616 | tf_op jit(solution)/shard_map/ppermute | solution.py:26
  291.5 57.7 %collective-permute-start.10 = (bf16[1,8,4096]{2,1,0:T(8,128)(2,1)}, bf16[1,8,4096]{2,1,0:T(8,128)(2,1)}, u32[]{:S(2)}, u32[]{:S(2)}) collective-permute-start(bf16[1,8,4096]{2,1,0:T(8,128)(2,1)} %fusion.54), channel_id=1, source_target_pairs={{1,0},{2,1},{3,2},{4,3},{5,4},{6,5},{7,6},{9,8},{10,9},{11,10},{12... | collective-permute-start | bytes 196616 | tf_op jit(solution)/shard_map/ppermute | solution.py:29
  293.4 50.8 %collective-permute-start.8 = (bf16[1,8,4096]{2,1,0:T(8,128)(2,1)}, bf16[1,8,4096]{2,1,0:T(8,128)(2,1)}, u32[]{:S(2)}, u32[]{:S(2)}) collective-permute-start(bf16[1,8,4096]{2,1,0:T(8,128)(2,1)} %fusion.52), channel_id=1, source_target_pairs={{8,0},{16,8},{24,16},{32,24},{40,32},{48,40},{56,48},{64,56},{72,6... | collective-permute-start | bytes 196616 | tf_op jit(solution)/shard_map/ppermute | solution.py:29
  294.7 44.6 %collective-permute-start.11 = (bf16[1,8,4096]{2,1,0:T(8,128)(2,1)}, bf16[1,8,4096]{2,1,0:T(8,128)(2,1)}, u32[]{:S(2)}, u32[]{:S(2)}) collective-permute-start(bf16[1,8,4096]{2,1,0:T(8,128)(2,1)} %fusion.55), channel_id=1, source_target_pairs={{0,1},{1,2},{2,3},{3,4},{4,5},{5,6},{6,7},{8,9},{9,10},{10,11},{11... | collective-permute-start | bytes 196616 | tf_op jit(solution)/shard_map/ppermute | solution.py:26
  314.3 6.5 %copy-start.17 = (f32[8,64,1,2,2,1,4,4]{1,7,6,5,4,3,2,0:T(4,128)S(1)}, f32[8,64,1,2,2,1,4,4]{1,7,6,5,4,3,2,0:T(4,128)}, u32[]{:S(2)}) copy-start(f32[8,64,1,2,2,1,4,4]{1,7,6,5,4,3,2,0:T(4,128)} %copy.165) | copy-start | bytes 393220
  314.3 6.7 %copy-start.19 = (f32[8,64,1,2,2,1,4,4]{1,7,6,5,4,3,2,0:T(4,128)S(1)}, f32[8,64,1,2,2,1,4,4]{1,7,6,5,4,3,2,0:T(4,128)}, u32[]{:S(2)}) copy-start(f32[8,64,1,2,2,1,4,4]{1,7,6,5,4,3,2,0:T(4,128)} %copy.169) | copy-start | bytes 393220
  314.3 6.8 %copy-start.16 = (f32[8,64,2,1,2,4,1,4]{1,7,6,5,4,3,2,0:T(4,128)S(1)}, f32[8,64,2,1,2,4,1,4]{1,7,6,5,4,3,2,0:T(4,128)}, u32[]{:S(2)}) copy-start(f32[8,64,2,1,2,4,1,4]{1,7,6,5,4,3,2,0:T(4,128)} %copy.173) | copy-start | bytes 393220
  339.0 218.4 %all-reduce.13.cloned.1.call-start = ((), (), s32[]{:S(2)}) async-start(), calls=%async_computation.1 | async-start | bytes 917504 | tf_op jit(solution)/shard_map/psum | solution.py:6
  359.4 134.4 %copy-start.31 = (pred[8]{0:T(512)(128)(4,1)S(1)}, pred[8]{0:T(512)(128)(4,1)}, u32[]{:S(2)}) copy-start(pred[8]{0:T(512)(128)(4,1)} %copy-done.30) | copy-start | bytes 28
  493.8 68.4 %copy-start.1 = (bf16[128,512]{1,0:T(8,128)(2,1)S(1)}, bf16[128,512]{1,0:T(8,128)(2,1)}, u32[]{:S(2)}) copy-start(bf16[128,512]{1,0:T(8,128)(2,1)} %param.32) | copy-start | bytes 393220
  (26 other events, 53.8 us)
Sparse Core Ops, SparseCore 0:
  339.1 154.6 all-reduce.10
  496.3 61.0 all-reduce.12
